TPU v7x, 256 devices: a whole 4x4x8 slice. The times are simulated.
256 devices in a mesh: dp: 8 (over z_hi, core), expert: 32 (over z_lo, y, x).
Axes of the slice: x: 4, y: 4, z: 8 (z_hi: 4, z_lo: 2; z = z_hi * 2 + z_lo), core: 2. Of those that a mesh axis runs over, the one named last changes fastest.
Arguments:
- tokens: bfloat16 [32768, 1152], P(('dp', 'expert')), may hold values from -6 to 6
- out_grad: bfloat16 [32768, 1152], P(('dp', 'expert')), may hold values from -6 to 6
- gates: float32 [32768, 2], P(('dp', 'expert')), may hold values from 0.05 to 1
- expert_ids: int32 [32768, 2], P(('dp', 'expert')), may hold values from 0 to 31, all different within a row; in each aligned block of 128 rows (0 to 127, 128 to 255, ...) at most 12 rows name the same one
- swap_list: int32 [32], replicated, may hold values from 0 to 31, as said below
- w_in: bfloat16 [32, 1152, 3072], P('expert', None, 'dp'), may hold values from -0.1875 to 0.1875
- w_out: bfloat16 [32, 3072, 1152], P('expert', 'dp'), may hold values from -0.109375 to 0.109375
- first_moment: float32 [32, 1152, 3072], P('expert', None, 'dp'), may hold values from -12 to 12
- second_moment: float32 [32, 1152, 3072], P('expert', None, 'dp'), may hold values from 1 to 100
Outputs:
- x_grad: bfloat16 [32768, 1152], P(('dp', 'expert'))
- adam_out: bfloat16 [32, 1152, 3072], P('expert', None, 'dp')
Inputs may be any that keep to these rules, and one draw needn't show every extreme that they name: `expert_ids`: among the 128 tokens of one device no expert is named by more than 12 rows; a token's two experts differ. swap_list[e] is e or e XOR 32/2, and swap_list[swap_list[e]] = e; swap_list[0] = 16 and swap_list[31] = 15.
All inputs are finite; a program needn't handle non-finite values.
Results may differ from a plain program's by a relative error of at most 0.015.
Values may be sent and summed in bfloat16 or wider, within the bound.
A program may use at most 128 MiB of HBM per device.

v0:
```python
import jax
import jax.numpy as jnp
from jax import lax
from jax.sharding import PartitionSpec as P

ADAM_STEP = 100


coef_c = 0.7978845608028654
coef_a = 0.044715
beta_one = 0.9
beta_two = 0.999
adam_eps = 1e-08


def partner(block, axis, apart):
    count = lax.axis_size(axis)
    route = []
    for low in range(count):
        high = low | 1 << apart
        if high != low and high < count:
            route += [(low, high), (high, low)]
    return lax.ppermute(block, axis, route)


def gelu_slope(pre_act):
    inner_arg = coef_c * (pre_act + coef_a * pre_act * pre_act * pre_act)
    tanh_val = jnp.tanh(inner_arg)
    return 0.5 * (1.0 + tanh_val) + 0.5 * pre_act * (1.0 - tanh_val * tanh_val) * coef_c * (
        1.0 + 3.0 * coef_a * pre_act * pre_act
    )


def pack_rows(id_block, x_block, g_block, dest_table, capacity):
    expert_count = dest_table.shape[0]
    flat_ids = id_block.reshape(-1)
    assigned = flat_ids.shape[0]
    lane_ids = jnp.arange(expert_count, dtype=jnp.int32)
    id_onehot = (flat_ids[:, None] == lane_ids[None, :]).astype(jnp.int32)
    dest_dev = jnp.sum(id_onehot * dest_table[None, :], axis=1)
    onehot = (dest_dev[:, None] == lane_ids[None, :]).astype(jnp.int32)
    before = jnp.cumsum(onehot, axis=0) - onehot
    slot_idx = jnp.sum(before * onehot, axis=1)
    where_to = dest_dev * capacity + slot_idx
    source = (
        jnp.zeros((expert_count * capacity,), jnp.int32)
        .at[where_to]
        .set(jnp.arange(assigned, dtype=jnp.int32) + 1)
    )
    filled = (source > 0)[:, None]
    pick_idx = jnp.maximum(source - 1, 0)
    model_width = x_block.shape[1]
    x_rows = jnp.where(
        filled, jnp.take(x_block, pick_idx // 2, axis=0), jnp.zeros((), jnp.bfloat16)
    )
    g_rows = jnp.where(
        filled,
        jnp.take(g_block.reshape(assigned, model_width), pick_idx, axis=0),
        jnp.zeros((), jnp.bfloat16),
    )
    return (
        x_rows.reshape(expert_count, capacity, model_width),
        g_rows.reshape(expert_count, capacity, model_width),
        where_to,
    )


def shards(
    tokens, out_grad, gates, expert_ids, swap_list, w_in, w_out, first_moment, second_moment
):
    expert_count = lax.axis_size("expert")
    top_bit = expert_count.bit_length() - 2
    own_index = lax.axis_index("expert")
    lane_ids = jnp.arange(expert_count, dtype=jnp.int32)
    partner_me = jnp.sum(jnp.where(lane_ids == own_index, swap_list, 0))
    is_moved = partner_me != own_index
    tok_count = tokens.shape[0]
    model_width = tokens.shape[1]
    capacity = 3 * tok_count // expert_count
    grad_pair = (gates[:, :, None] * out_grad[:, None, :].astype(jnp.float32)).astype(jnp.bfloat16)
    swapped = (
        partner(w_in, "expert", top_bit),
        partner(w_out, "expert", top_bit),
        partner(first_moment.astype(jnp.bfloat16), "expert", top_bit).astype(first_moment.dtype),
        partner(second_moment.astype(jnp.bfloat16), "expert", top_bit).astype(second_moment.dtype),
    )
    w_in = jnp.where(is_moved, swapped[0], w_in)
    w_out = jnp.where(is_moved, swapped[1], w_out)
    first_moment = jnp.where(is_moved, swapped[2], first_moment)
    second_moment = jnp.where(is_moved, swapped[3], second_moment)
    x_buf, g_buf, where_to = pack_rows(expert_ids, tokens, grad_pair, swap_list, capacity)
    x_recv, g_recv = (
        lax.all_to_all(x_buf, "expert", split_axis=0, concat_axis=0, tiled=True),
        lax.all_to_all(g_buf, "expert", split_axis=0, concat_axis=0, tiled=True),
    )
    x_all, g_all = (
        lax.all_gather(x_recv, "dp", axis=0, tiled=True),
        lax.all_gather(g_recv, "dp", axis=0, tiled=True),
    )
    x_rows = x_all.reshape(-1, model_width)
    g_rows = g_all.reshape(-1, model_width)
    w_in_local = w_in[0]
    w_out_local = w_out[0]
    pre_act = jnp.dot(x_rows, w_in_local, preferred_element_type=jnp.float32)
    act_grad = lax.dot_general(
        g_rows, w_out_local, (((1,), (1,)), ((), ())), preferred_element_type=jnp.float32
    )
    pre_grad = (act_grad * gelu_slope(pre_act)).astype(jnp.bfloat16)
    own_rows = lax.psum_scatter(
        lax.dot_general(
            pre_grad, w_in_local, (((1,), (1,)), ((), ())), preferred_element_type=jnp.float32
        ).astype(jnp.bfloat16),
        "dp",
        scatter_dimension=0,
        tiled=True,
    )
    returned = lax.all_to_all(
        own_rows.reshape(expert_count, capacity, model_width),
        "expert",
        split_axis=0,
        concat_axis=0,
        tiled=True,
    )
    picked = jnp.take(
        returned.reshape(expert_count * capacity, model_width), where_to, axis=0
    ).astype(jnp.float32)
    x_grad = jnp.sum(picked.reshape(tok_count, 2, model_width), axis=1).astype(jnp.bfloat16)
    weight_grad = lax.dot_general(
        x_rows, pre_grad, (((0,), (0,)), ((), ())), preferred_element_type=jnp.float32
    )
    first_new = beta_one * first_moment[0] + (1.0 - beta_one) * weight_grad
    second_new = beta_two * second_moment[0] + (1.0 - beta_two) * weight_grad * weight_grad
    adam_out = (
        first_new
        / (1.0 - beta_one**ADAM_STEP)
        / (jnp.sqrt(second_new / (1.0 - beta_two**ADAM_STEP)) + adam_eps)
    )
    adam_out = adam_out.astype(jnp.bfloat16)[None]
    return (x_grad, adam_out)


def solution(mesh):
    in_specs = (
        P(("dp", "expert"), None),
        P(("dp", "expert"), None),
        P(("dp", "expert"), None),
        P(("dp", "expert"), None),
        P(),
        P("expert", None, "dp"),
        P("expert", "dp", None),
        P("expert", None, "dp"),
        P("expert", None, "dp"),
    )
    out_specs = (P(("dp", "expert"), None), P("expert", None, "dp"))
    return jax.shard_map(shards, mesh=mesh, in_specs=in_specs, out_specs=out_specs, check_vma=False)
```

profile of v0, /device:TPU:1, one launch (start us, length us, event | category | flops | bytes accessed | tf_op | source)
XLA Modules:
  0.0 421.6 jit_solution(744545004526713579)
XLA Ops:
  13.3 2.2 gather_fusion.1
  18.0 2.2 gather_fusion
  21.8 1.7 select_select_fusion.1
  23.6 27.0 %all_to_all.15 = bf16[32,12,1152]{2,1,0:T(8,128)(2,1)S(1)} all-to-all(bf16[32,12,1152]{2,1,0:T(8,128)(2,1)S(1)} %get-tuple-element.5), channel_id=1, replica_groups=mesh['dp'=8,'expert'=32] {'expert'}, dimensions={0} | all-to-all | bytes 1769472 | tf_op jit(solution)/shard_map/all_to_all | solution.py:93
  51.8 33.8 %all_to_all.16 = bf16[32,12,1152]{2,1,0:T(8,128)(2,1)S(1)} all-to-all(bf16[32,12,1152]{2,1,0:T(8,128)(2,1)S(1)} %get-tuple-element.4), channel_id=1, replica_groups=mesh['dp'=8,'expert'=32] {'expert'}, dimensions={0} | all-to-all | bytes 1769472 | tf_op jit(solution)/shard_map/all_to_all | solution.py:94
  86.8 3.0 collective-permute-start.1
  91.4 63.6 %all-gather.5.cloned.1.call-done = bf16[256,12,1152]{2,0,1:T(8,128)(2,1)} async-done(((bf16[32,12,1152]{2,0,1:T(8,128)(2,1)}), bf16[256,12,1152]{2,0,1:T(8,128)(2,1)}) %all-gather.5.cloned.1.call-update) | async-done | bytes 7077904 | tf_op jit(solution)/shard_map/all_gather | solution.py:97
  155.0 10.9 %copy.20 = bf16[256,12,1152]{2,1,0:T(8,128)(2,1)} copy(bf16[256,12,1152]{2,0,1:T(8,128)(2,1)} %all-gather.5.cloned.1.call-done) | data formatting | bytes 14155776 | tf_op jit(solution)/shard_map/all_gather | solution.py:97
  165.9 12.1 %reshape.124 = bf16[3072,1152]{1,0:T(8,128)(2,1)} reshape(bf16[256,12,1152]{2,1,0:T(8,128)(2,1)} %copy.20) | data formatting | bytes 14155776 | tf_op jit(solution)/shard_map/reshape | solution.py:100
  178.0 46.5 %all-gather.3.cloned.1.call-done = bf16[256,12,1152]{2,0,1:T(8,128)(2,1)} async-done(((bf16[32,12,1152]{2,0,1:T(8,128)(2,1)}), bf16[256,12,1152]{2,0,1:T(8,128)(2,1)}) %all-gather.3.cloned.1.call-update) | async-done | bytes 7077904 | tf_op jit(solution)/shard_map/all_gather | solution.py:98
  224.5 10.9 %copy.18 = bf16[256,12,1152]{2,1,0:T(8,128)(2,1)} copy(bf16[256,12,1152]{2,0,1:T(8,128)(2,1)} %all-gather.3.cloned.1.call-done) | data formatting | bytes 14155776 | tf_op jit(solution)/shard_map/all_gather | solution.py:98
  235.4 11.8 %reshape.123 = bf16[3072,1152]{1,0:T(8,128)(2,1)} reshape(bf16[256,12,1152]{2,1,0:T(8,128)(2,1)} %copy.18) | data formatting | bytes 14155776 | tf_op jit(solution)/shard_map/reshape | solution.py:101
  247.2 6.5 %fusion.15 = f32[3072,384]{1,0:T(8,128)S(1)} fusion(bf16[3072,1152]{1,0:T(8,128)(2,1)} %reshape.124, bf16[1,1152,384]{2,1,0:T(8,128)(2,1)S(1)} %collective-permute-done.1, bf16[1,1152,384]{2,1,0:T(8,128)(2,1)S(1)} %copy-done.12, pred[]{:T(512)S(6)} %ne.17), kind=kOutput, calls=%fused_computation.28 | convolution fusion | flops 2718351360 | bytes 13565953 | tf_op jit(solution)/shard_map/dot_general | solution.py:104
  253.7 7.9 %fusion.6 = bf16[3072,384]{1,0:T(8,128)(2,1)S(1)} fusion(f32[3072,384]{1,0:T(8,128)S(1)} %fusion.15, bf16[3072,1152]{1,0:T(8,128)(2,1)S(1)} %copy-done.2, bf16[1,384,1152]{2,1,0:T(8,128)(2,1)} %collective-permute-done, bf16[1,384,1152]{2,1,0:T(8,128)(2,1)S(1)} %copy-done.11, pred[]{:T(512)S(6)} %ne.17), kind=kOutput, calls=%fused_computation.13 | convolution fusion | flops 2740764672 | bytes 15925249 | tf_op jit(solution)/shard_map/dot_general | solution.py:105
  261.6 1.4 copy-done.13
  263.0 6.1 %convolution_convert_fusion = bf16[3072,1152]{1,0:T(8,128)(2,1)} fusion(bf16[3072,384]{1,0:T(8,128)(2,1)S(1)} %fusion.6, bf16[1,1152,384]{2,1,0:T(8,128)(2,1)S(1)} %collective-permute-done.1, bf16[1,1152,384]{2,1,0:T(8,128)(2,1)S(1)} %copy-done.12, pred[]{:T(512)S(6)} %ne.17), kind=kOutput, calls=%fused_computation.4 | convolution fusion | flops 2721890304 | bytes 11206657 | tf_op jit(solution)/shard_map/dot_general | solution.py:110
  269.2 1.4 copy-done.4
  270.7 8.7 %collective-permute-start.3 = (bf16[1,1152,384]{2,1,0:T(8,128)(2,1)S(1)}, bf16[1,1152,384]{2,1,0:T(8,128)(2,1)}, u32[]{:S(2)}, u32[]{:S(2)}) collective-permute-start(bf16[1,1152,384]{2,1,0:T(8,128)(2,1)S(1)} %convert_element_type.48), channel_id=1, source_target_pairs={{0,16},{16,0},{1,17},{17,1},{2,18},{18,2},{3,19},{19,3},{4,20},{20... | collective-permute-start | bytes 2654216 | tf_op jit(solution)/shard_map/ppermute | solution.py:23
  280.9 107.0 %reduce-scatter.2.cloned.1.call-done = bf16[384,1152]{1,0:T(8,128)(2,1)} async-done(((bf16[3072,1152]{1,0:T(8,128)(2,1)}), bf16[384,1152]{1,0:T(8,128)(2,1)}) %reduce-scatter.2.cloned.1.call-update) | async-done | bytes 884752 | tf_op jit(solution)/shard_map/reduce_scatter | solution.py:109
  387.9 2.2 reshape.125
  390.1 7.8 %all-to-all-start.2 = ((bf16[32,12,1152]{2,1,0:T(8,128)(2,1)}), bf16[32,12,1152]{2,1,0:T(8,128)(2,1)S(1)}, u32[]{:S(2)}, u32[]{:S(2)}) async-start(bf16[32,12,1152]{2,1,0:T(8,128)(2,1)} %reshape.125), calls=%async_computation.3 | async-start | bytes 2359296 | tf_op jit(solution)/shard_map/all_to_all | solution.py:117
  398.1 10.0 %fusion.20 = bf16[1,1152,384]{2,1,0:T(8,128)(2,1)} fusion(f32[1,1152,384]{2,1,0:T(8,128)} %param.17, bf16[1,1152,384]{2,1,0:T(8,128)(2,1)} %collective-permute-done.3, f32[1,1152,384]{2,1,0:T(8,128)} %param.16, bf16[1,1152,384]{2,1,0:T(8,128)(2,1)} %collective-permute-done.2, pred[]{:T(512)S(6)} %ne.17, bf16[3072,1152]{1,0:T(8,128)(2,1)} %reshape.124, ...), kind=kOutput, calls=%fused_computation.34 | convolution fusion | flops 2724986880 | bytes 15630337 | tf_op jit(solution)/shard_map/dot_general | solution.py:128
  408.1 3.1 all-to-all-done.2
  413.0 2.1 fusion.21
  (76 shorter events, 16.8 us)
Async XLA Ops:
  7.2 6.1 %copy-start = (bf16[128,1152]{1,0:T(8,128)(2,1)S(1)}, bf16[128,1152]{1,0:T(8,128)(2,1)}, u32[]{:S(2)}) copy-start(bf16[128,1152]{1,0:T(8,128)(2,1)} %param.9) | copy-start | bytes 884740
  7.2 147.8 %all-gather.5.cloned.1.call-start = ((), (), s32[]{:S(2)}) async-start(), calls=%async_computation.5 | async-start | bytes 7962624 | tf_op jit(solution)/shard_map/all_gather | solution.py:97
  9.9 1.4 copy-start.8
  13.2 3.5 copy-start.6
  17.0 1.0 copy-start.7
  20.2 1.6 copy-start.3
  51.7 172.8 %all-gather.3.cloned.1.call-start = ((), (), s32[]{:S(2)}) async-start(), calls=%async_computation.4 | async-start | bytes 7962624 | tf_op jit(solution)/shard_map/all_gather | solution.py:98
  51.8 35.0 %copy-start.12 = (bf16[1,1152,384]{2,1,0:T(8,128)(2,1)S(1)}, bf16[1,1152,384]{2,1,0:T(8,128)(2,1)}, u32[]{:S(2)}) copy-start(bf16[1,1152,384]{2,1,0:T(8,128)(2,1)} %param.14) | copy-start | bytes 2654212
  51.8 38.1 %copy-start.11 = (bf16[1,384,1152]{2,1,0:T(8,128)(2,1)S(1)}, bf16[1,384,1152]{2,1,0:T(8,128)(2,1)}, u32[]{:S(2)}) copy-start(bf16[1,384,1152]{2,1,0:T(8,128)(2,1)} %param.15) | copy-start | bytes 2654212
  51.8 38.3 %copy-start.10 = (s32[32]{0:T(128)S(1)}, s32[32]{0:T(128)}, u32[]{:S(2)}) copy-start(s32[32]{0:T(128)} %param.13) | copy-start | bytes 388
  86.7 301.2 %reduce-scatter.2.cloned.1.call-start = ((), (), s32[]{:S(2)}) async-start(), calls=%async_computation.6 | async-start | bytes 7962624 | tf_op jit(solution)/shard_map/reduce_scatter | solution.py:109
  86.8 160.4 %collective-permute-start.1 = (bf16[1,1152,384]{2,1,0:T(8,128)(2,1)S(1)}, bf16[1,1152,384]{2,1,0:T(8,128)(2,1)S(1)}, u32[]{:S(2)}, u32[]{:S(2)}) collective-permute-start(bf16[1,1152,384]{2,1,0:T(8,128)(2,1)S(1)} %copy-done.12), channel_id=1, source_target_pairs={{0,16},{16,0},{1,17},{17,1},{2,18},{18,2},{3,19},{19,3},{4,20},{20... | collective-permute-start | bytes 2654216 | tf_op jit(solution)/shard_map/ppermute | solution.py:23
  89.8 163.8 %collective-permute-start = (bf16[1,384,1152]{2,1,0:T(8,128)(2,1)S(1)}, bf16[1,384,1152]{2,1,0:T(8,128)(2,1)}, u32[]{:S(2)}, u32[]{:S(2)}) collective-permute-start(bf16[1,384,1152]{2,1,0:T(8,128)(2,1)S(1)} %copy-done.11), channel_id=1, source_target_pairs={{0,16},{16,0},{1,17},{17,1},{2,18},{18,2},{3,19},{19,3},{4,20},{20... | collective-permute-start | bytes 2654216 | tf_op jit(solution)/shard_map/ppermute | solution.py:23
  247.2 6.5 %copy-start.2 = (bf16[3072,1152]{1,0:T(8,128)(2,1)S(1)}, bf16[3072,1152]{1,0:T(8,128)(2,1)}, u32[]{:S(2)}) copy-start(bf16[3072,1152]{1,0:T(8,128)(2,1)} %reshape.123) | copy-start | bytes 21233668
  261.6 1.5 copy-start.13
  269.2 1.5 copy-start.4
  270.6 8.8 %copy-start.5 = (f32[1,1152,384]{2,1,0:T(8,128)S(1)}, f32[1,1152,384]{2,1,0:T(8,128)}, u32[]{:S(2)}) copy-start(f32[1,1152,384]{2,1,0:T(8,128)} %param.16) | copy-start | bytes 5308420
  270.7 127.4 %collective-permute-start.3 = (bf16[1,1152,384]{2,1,0:T(8,128)(2,1)S(1)}, bf16[1,1152,384]{2,1,0:T(8,128)(2,1)}, u32[]{:S(2)}, u32[]{:S(2)}) collective-permute-start(bf16[1,1152,384]{2,1,0:T(8,128)(2,1)S(1)} %convert_element_type.48), channel_id=1, source_target_pairs={{0,16},{16,0},{1,17},{17,1},{2,18},{18,2},{3,19},{19,3},{4,20},{20... | collective-permute-start | bytes 2654216 | tf_op jit(solution)/shard_map/ppermute | solution.py:23
  279.5 118.5 %copy-start.9 = (s32[256,1]{0,1:T(1,128)S(1)}, s32[256,1]{0,1:T(1,128)}, u32[]{:S(2)}) copy-start(s32[256,1]{0,1:T(1,128)} %copy-done.8) | copy-start | bytes 3076
  279.5 118.6 %collective-permute-start.2 = (bf16[1,1152,384]{2,1,0:T(8,128)(2,1)S(1)}, bf16[1,1152,384]{2,1,0:T(8,128)(2,1)}, u32[]{:S(2)}, u32[]{:S(2)}) collective-permute-start(bf16[1,1152,384]{2,1,0:T(8,128)(2,1)S(1)} %convert_element_type.46), channel_id=1, source_target_pairs={{0,16},{16,0},{1,17},{17,1},{2,18},{18,2},{3,19},{19,3},{4,20},{20... | collective-permute-start | bytes 2654216 | tf_op jit(solution)/shard_map/ppermute | solution.py:23
  390.1 21.2 %all-to-all-start.2 = ((bf16[32,12,1152]{2,1,0:T(8,128)(2,1)}), bf16[32,12,1152]{2,1,0:T(8,128)(2,1)S(1)}, u32[]{:S(2)}, u32[]{:S(2)}) async-start(bf16[32,12,1152]{2,1,0:T(8,128)(2,1)} %reshape.125), calls=%async_computation.3 | async-start | bytes 2359296 | tf_op jit(solution)/shard_map/all_to_all | solution.py:117
  411.5 3.6 copy-start.1
Sparse Core Ops, SparseCore 0:
  51.8 103.0 all-gather.4
  156.8 67.6 all-gather.2
  269.3 118.5 reduce-scatter.1
where the time goes:
time: 426 us; the launch traced here: 422 us
  waiting for transfers between devices  220 us (52%)
  local copies, waits for them, and re-layouts  67 us (16%)
  blocking collectives  60.8 us (14%)
  matrix products  30.5 us (7%)
  starting transfers between devices  21.3 us (5%)
  between operations  14.8 us (3%)
  other arithmetic  6.92 us (2%)
    reduce_scatter x1, waiting for transfers between devices, shards(): lax.psum_scatter(lax.dot_general(pre_grad, w_in_local, (((1,), (1,)), (()...  107 us
    all_gather x1, waiting for transfers between devices, shards(): lax.all_gather(x_recv, 'dp', axis=0, tiled=True)  63.6 us
    all_gather x1, waiting for transfers between devices, shards(): lax.all_gather(g_recv, 'dp', axis=0, tiled=True)  46.5 us
    all_to_all x1, blocking collectives, shards(): lax.all_to_all(g_buf, 'expert', split_axis=0, concat_axis=0, tiled=True)  33.8 us
    all_to_all x1, blocking collectives, shards(): lax.all_to_all(x_buf, 'expert', split_axis=0, concat_axis=0, tiled=True)  27 us
    ppermute x4, starting transfers between devices, partner(): return lax.ppermute(block, axis, route)  13.4 us
    reshape x1, local copies, waits for them, and re-layouts, shards(): x_rows = x_all.reshape(-1, model_width)  12.1 us
    reshape x1, local copies, waits for them, and re-layouts, shards(): g_rows = g_all.reshape(-1, model_width)  11.8 us
  transfers between devices with their start and end apart: 8, of which 4 were waited for; matrix products, arithmetic and copies ran while one was open for 16% of the time, Pallas kernels for 0%

commit v1 on v0

v1 whole, which is shorter than its diff:
```python
import jax
import jax.numpy as jnp
from jax import lax
from jax.experimental import pallas as pl
from jax.experimental.pallas import tpu as pltpu
from jax.sharding import PartitionSpec as P

ADAM_STEP = 100
coef_c = 0.7978845608028654
coef_a = 0.044715
beta_one = 0.9
beta_two = 0.999
adam_eps = 1e-08

D = 1152
H = 384
T = 128
E = 32
CAP = 12
B = 2 * CAP
R = E * B
C = 384
MESH = pl.DeviceIdType.MESH
f32, bf16 = jnp.float32, jnp.bfloat16

INFO, XRAW, GRAW, WI, WO0, WO1, CWI, CWO, FWI, FWO0, FWO1, GC, GW, SWAP, BACK = (
    0, 1, 2, 3, 4, 5, 6, 7, 8, 9, 10, 11, 14, 17, 20,
)
N_ONE = 21
N_LOCAL = 9


def gelu_slope(u):
    h = jnp.tanh(coef_c * (u + coef_a * u * u * u))
    return 0.5 * (1.0 + h) + 0.5 * u * (1.0 - h * h) * coef_c * (
        1.0 + 3.0 * coef_a * u * u
    )


def dot(a, b):
    return jnp.dot(a, b, preferred_element_type=f32)


def dot_t(a, b):
    return lax.dot_general(a, b, (((1,), (1,)), ((), ())), preferred_element_type=f32)


def kernel(
    tok, og, ids, gts, win, wout, m1, m2,
    xo, xr, ao, ar,
    info, xraw, graw, pk, pt, xpk, gpk, xrv, grv, xt, sl, wi, wo, pg, rg, rt, wg, wsc, wrc, wsw, wrw, mm1, mm2, xs,
    s1, r1, lo, sx, rx, sg, rgs, st, rts,
):
    dp, e = lax.axis_index("dp"), lax.axis_index("expert")
    zh, core = dp // 2, dp % 2
    p_row = ((zh + 1 - 2 * (zh % 2)) * 2 + core, e)
    p_wgt = ((3 - zh) * 2 + core, e)
    p_core = (zh * 2 + 1 - core, e)
    p_swap = (dp, (e + E // 2) % E)

    def one(i, src, dst, dev):
        return pltpu.make_async_remote_copy(
            src_ref=src, dst_ref=dst, send_sem=s1.at[i], recv_sem=r1.at[i], device_id=dev, device_id_type=MESH
        )

    def local(i, src, dst):
        return pltpu.make_async_copy(src, dst, lo.at[i])

    def at_block(ref, q):
        return ref.at[q]

    def rows_of(ref, i, n):
        return ref[pl.ds(i * n, n)].reshape(n * B, D)

    def put_rows(ref, i, n, value):
        ref[pl.ds(i * n, n)] = value.astype(bf16).reshape(n, B, D)

    def send(src, dst, ss, rs, d):
        q = (e + d) % E
        return pltpu.make_async_remote_copy(
            src_ref=at_block(src, q), dst_ref=at_block(dst, e), send_sem=ss.at[d], recv_sem=rs.at[d],
            device_id=(dp, q), device_id_type=MESH,
        )

    def arrival(src, dst, ss, rs, d):
        q = (e + E - d) % E
        return pltpu.make_async_remote_copy(
            src_ref=at_block(src, q), dst_ref=at_block(dst, q), send_sem=ss.at[d], recv_sem=rs.at[d],
            device_id=(dp, q), device_id_type=MESH,
        )

    def send_all(src, dst, ss, rs, own):
        own.start()

        @pl.loop(1, E)
        def _(d):
            send(src, dst, ss, rs, d).start()

    def wait_all(src, dst, ss, rs, own):
        own.wait()

        @pl.loop(1, E)
        def _(d):
            arrival(src, dst, ss, rs, d).wait_recv()

    copies = [
        local(0, tok, xraw.at[pl.ds(0, T)]),
        local(1, og, graw.at[pl.ds(0, T)]),
        local(2, win.at[0], wi.at[:, pl.ds(0, H)]),
        local(3, wout.at[0], wo.at[pl.ds(0, H)]),
        local(4, m1.at[0], mm1),
        local(5, m2.at[0], mm2),
    ]
    for c in copies:
        c.start()

    iota_r = lax.broadcasted_iota(jnp.int32, (T, T), 0)
    iota_c = lax.broadcasted_iota(jnp.int32, (T, T), 1)
    eye, before = iota_r == iota_c, iota_r < iota_c
    idr = [ids[k : k + 1, :].astype(f32) for k in range(2)]

    def to_col(row):
        return jnp.sum(jnp.where(eye, row, 0.0), axis=1, keepdims=True)

    idc = [to_col(r) for r in idr]

    def count(k, j, mask):
        same = idc[k] == idr[j]
        same = jnp.logical_and(same, mask) if mask is not None else same
        return jnp.sum(jnp.where(same, 1.0, 0.0), axis=0, keepdims=True)

    rank0 = count(0, 0, before)
    rank1 = count(0, 1, None) + count(1, 1, before)
    info[0, 0:1, :] = idr[0] * float(B) + rank0
    info[0, 1:2, :] = idr[1] * float(B) + rank1
    info[0, 2:4, :] = gts[...]
    info[0, 4:8, :] = jnp.zeros((4, T), f32)

    barrier = pltpu.get_barrier_semaphore()
    for dev in (p_row, p_wgt, p_core):
        pl.semaphore_signal(barrier, inc=1, device_id=dev, device_id_type=MESH)

    @pl.loop(1, E)
    def _(d):
        pl.semaphore_signal(barrier, inc=1, device_id=(dp, (e + d) % E), device_id_type=MESH)

    pl.semaphore_wait(barrier, E + 2)

    c_info = one(INFO, info.at[0], info.at[1], p_row)
    c_x = one(XRAW, tok, xraw.at[pl.ds(T, T)], p_row)
    c_g = one(GRAW, og, graw.at[pl.ds(T, T)], p_row)
    half = H // 2
    c_wi = one(WI, win.at[0], wi.at[:, pl.ds(2 * H, H)], p_wgt)
    c_wo = [
        one(WO0 + i, wout.at[0, pl.ds(i * half, half)], wo.at[pl.ds(2 * H + i * half, half)], p_wgt)
        for i in range(2)
    ]
    c_cwi = one(CWI, win.at[0], wi.at[:, pl.ds(H, H)], p_core)
    c_cwo = one(CWO, wout.at[0], wo.at[pl.ds(H, H)], p_core)
    early = [c_info, c_x, c_g, c_wi, *c_wo, c_cwi, c_cwo]
    for c in early:
        c.start()

    def build(src):
        code = info[src, 0:2, :] + float(CAP * src)
        row = lax.broadcasted_iota(jnp.int32, (R, T), 0).astype(f32)
        hit = jnp.logical_or(row == code[0:1, :], row == code[1:2, :])
        pk[:, src * T : (src + 1) * T] = jnp.where(hit, 1.0, 0.0).astype(bf16)
        lane = lax.broadcasted_iota(jnp.int32, (T, R), 1).astype(f32)
        hit = jnp.logical_or(lane == to_col(code[0:1, :]), lane == to_col(code[1:2, :]))
        pt[src * T : (src + 1) * T, :] = jnp.where(hit, 1.0, 0.0).astype(bf16)

    build(0)
    for c in copies[:2]:
        c.wait()
    c_info.wait_recv()
    build(1)
    tile = R // 4

    c_x.wait_recv()

    @pl.loop(0, 4)
    def _(i):
        rows = pl.ds(pl.multiple_of(i * tile, tile), tile)
        put_rows(xpk, i, E // 4, dot(pk[rows, :], xraw[...]))

    own_x = local(6, at_block(xpk, e), at_block(xrv, e))
    send_all(xpk, xrv, sx, rx, own_x)

    c_g.wait_recv()

    @pl.loop(0, 4)
    def _(i):
        rows = pl.ds(pl.multiple_of(i * tile, tile), tile)
        row = (lax.broadcasted_iota(jnp.int32, (tile, T), 0) + i * tile).astype(f32)
        gate = jnp.zeros((tile, T), f32)
        for src in range(2):
            for k in range(2):
                hit = row == info[src, k : k + 1, :] + float(CAP * src)
                gate += jnp.where(hit, info[src, 2 + k : 3 + k, :], 0.0)
        gate = jnp.sum(gate, axis=1, keepdims=True)
        put_rows(gpk, i, E // 4, dot(pk[rows, :], graw[...]) * gate)

    own_g = local(7, at_block(gpk, e), at_block(grv, e))
    send_all(gpk, grv, sg, rgs, own_g)

    big, blocks = R // 2, E // 2

    def slopes(h):
        @pl.loop(0, R // big)
        def _(i):
            rows = pl.ds(pl.multiple_of(i * big, big), big)
            cols = slice(h * 2 * H, (h + 1) * 2 * H)
            sl[rows, cols] = gelu_slope(dot(rows_of(xrv, i, blocks), wi[:, cols]))

    def grads(h):
        @pl.loop(0, R // big)
        def _(i):
            rows = pl.ds(pl.multiple_of(i * big, big), big)
            cols = slice(h * 2 * H, (h + 1) * 2 * H)
            act = dot_t(rows_of(grv, i, blocks), wo[cols, :])
            pg[rows, cols] = (act * sl[rows, cols]).astype(bf16)

    copies[2].wait()
    c_cwi.wait_recv()
    wait_all(xpk, xrv, sx, rx, own_x)
    slopes(0)
    xt[...] = rows_of(xrv, 0, E).T
    c_wi.wait_recv()
    f_wi = one(FWI, wi.at[:, pl.ds(2 * H, H)], wi.at[:, pl.ds(3 * H, H)], p_core)
    f_wi.start()
    f_wi.wait_recv()
    slopes(1)
    copies[3].wait()
    c_cwo.wait_recv()
    wait_all(gpk, grv, sg, rgs, own_g)
    grads(0)
    f_wo = [
        one(FWO0 + i, wo.at[pl.ds(2 * H + i * half, half)], wo.at[pl.ds(3 * H + i * half, half)], p_core)
        for i in range(2)
    ]
    for i in range(2):
        c_wo[i].wait_recv()
        f_wo[i].start()
    for i in range(2):
        f_wo[i].wait_recv()
    grads(1)

    @pl.loop(0, 4)
    def _(i):
        rows = pl.ds(pl.multiple_of(i * tile, tile), tile)
        put_rows(rg, i, E // 4, dot_t(pg[rows, :], wi[...]))

    own_r = local(8, at_block(rg, e), at_block(rt, e))
    send_all(rg, rt, st, rts, own_r)

    n_chunks = D // C
    c_gc = [one(GC + i, wsc.at[pl.ds(i * C, C)], wrc.at[pl.ds(i * C, C)], p_core) for i in range(n_chunks)]
    c_gw = [one(GW + i, wsw.at[pl.ds(i * C, C)], wrw.at[pl.ds(i * C, C)], p_wgt) for i in range(n_chunks)]
    c_sw = [one(SWAP + i, ao.at[pl.ds(i * C, C)], ar.at[pl.ds(i * C, C)], p_swap) for i in range(n_chunks)]

    def partial_grad(i):
        rows = slice(i * C, (i + 1) * C)
        part = dot(xt[rows, :], pg[...])
        wg[rows, 0:H] = part[:, 0:H]
        wg[rows, H : 2 * H] = part[:, 2 * H : 3 * H]
        wsc[rows, 0:H] = part[:, H : 2 * H].astype(bf16)
        wsc[rows, H : 2 * H] = part[:, 3 * H : 4 * H].astype(bf16)
        c_gc[i].start()

    def pass_on(i):
        rows = slice(i * C, (i + 1) * C)
        c_gc[i].wait_recv()
        wsw[rows, :] = (wg[rows, H : 2 * H] + wrc[rows, H : 2 * H].astype(f32)).astype(bf16)
        c_gw[i].start()

    def adam(i):
        rows = slice(i * C, (i + 1) * C)
        c_gw[i].wait_recv()
        grad = wg[rows, 0:H] + wrc[rows, 0:H].astype(f32) + wrw[rows, :].astype(f32)
        first = beta_one * mm1[rows, :] + (1.0 - beta_one) * grad
        second = beta_two * mm2[rows, :] + (1.0 - beta_two) * grad * grad
        step = (first / (1.0 - beta_one**ADAM_STEP)) / (
            jnp.sqrt(second / (1.0 - beta_two**ADAM_STEP)) + adam_eps
        )
        ao[rows, :] = step.astype(bf16)
        c_sw[i].start()

    partial_grad(0)
    for i in range(1, n_chunks):
        partial_grad(i)
        pass_on(i - 1)
    pass_on(n_chunks - 1)

    for c in copies[4:]:
        c.wait()
    for i in range(n_chunks - 1):
        adam(i)

    wait_all(rg, rt, st, rts, own_r)
    xs[...] = dot(pt[T : 2 * T, :], rows_of(rt, 0, E)).astype(bf16)
    c_back = one(BACK, xs, xr, p_row)
    c_back.start()
    xo[...] = dot(pt[0:T, :], rows_of(rt, 0, E))
    adam(n_chunks - 1)

    @pl.loop(1, E)
    def _(d):
        send(xpk, xrv, sx, rx, d).wait_send()
        send(gpk, grv, sg, rgs, d).wait_send()
        send(rg, rt, st, rts, d).wait_send()

    for c in [*early, f_wi, *f_wo, *c_gc, *c_gw]:
        c.wait_send()
    for c in [*c_sw, c_back]:
        c.wait()


def shards(tokens, out_grad, gates, expert_ids, swap_list, w_in, w_out, first_moment, second_moment):
    any_spec = pl.BlockSpec(memory_space=pl.ANY)
    vmem = pl.BlockSpec(memory_space=pltpu.VMEM)
    dma = pltpu.SemaphoreType.DMA
    xo, xr, ao, ar = pl.pallas_call(
        kernel,
        out_shape=(
            jax.ShapeDtypeStruct((T, D), f32),
            jax.ShapeDtypeStruct((T, D), bf16),
            jax.ShapeDtypeStruct((D, H), bf16),
            jax.ShapeDtypeStruct((D, H), bf16),
        ),
        in_specs=[any_spec, any_spec, vmem, vmem, any_spec, any_spec, any_spec, any_spec],
        out_specs=(vmem, any_spec, vmem, any_spec),
        scratch_shapes=[
            pltpu.VMEM((2, 8, T), f32),
            pltpu.VMEM((2 * T, D), bf16),
            pltpu.VMEM((2 * T, D), bf16),
            pltpu.VMEM((R, 2 * T), bf16),
            pltpu.VMEM((2 * T, R), bf16),
            pltpu.VMEM((E, B, D), bf16),
            pltpu.VMEM((E, B, D), bf16),
            pltpu.VMEM((E, B, D), bf16),
            pltpu.VMEM((E, B, D), bf16),
            pltpu.VMEM((D, R), bf16),
            pltpu.VMEM((R, 4 * H), f32),
            pltpu.VMEM((D, 4 * H), bf16),
            pltpu.VMEM((4 * H, D), bf16),
            pltpu.VMEM((R, 4 * H), bf16),
            pltpu.VMEM((E, B, D), bf16),
            pltpu.VMEM((E, B, D), bf16),
            pltpu.VMEM((D, 2 * H), f32),
            pltpu.VMEM((D, 2 * H), bf16),
            pltpu.VMEM((D, 2 * H), bf16),
            pltpu.VMEM((D, H), bf16),
            pltpu.VMEM((D, H), bf16),
            pltpu.VMEM((D, H), f32),
            pltpu.VMEM((D, H), f32),
            pltpu.VMEM((T, D), bf16),
            dma((N_ONE,)), dma((N_ONE,)), dma((N_LOCAL,)),
            dma((E,)), dma((E,)), dma((E,)), dma((E,)), dma((E,)), dma((E,)),
        ],
        compiler_params=pltpu.CompilerParams(
            collective_id=0, has_side_effects=True, vmem_limit_bytes=60 << 20
        ),
        name="experts",
    )(tokens, out_grad, expert_ids.T, gates.T, w_in, w_out, first_moment, second_moment)
    x_grad = (xo + xr.astype(f32)).astype(bf16)
    own = lax.axis_index("expert")
    moved = jnp.sum(jnp.where(jnp.arange(E, dtype=jnp.int32) == own, swap_list, 0)) != own
    return x_grad, jnp.where(moved, ar, ao)[None]


def solution(mesh):
    token_spec = P(("dp", "expert"), None)
    in_specs = (
        token_spec, token_spec, token_spec, token_spec, P(),
        P("expert", None, "dp"), P("expert", "dp", None), P("expert", None, "dp"), P("expert", None, "dp"),
    )
    out_specs = (token_spec, P("expert", None, "dp"))
    return jax.shard_map(shards, mesh=mesh, in_specs=in_specs, out_specs=out_specs, check_vma=False)
```

time: 426 us -> 214 us (0.50)
  the two profiles are of different devices: /device:TPU:1 before, /device:TPU:127 now
where the time goes in v1:
time: 214 us
  Pallas kernels  207 us (97%)
  other arithmetic  5.46 us (3%)
    pallas_call x1, Pallas kernels, shards(): pl.pallas_call(kernel, out_shape=(jax.ShapeDtypeStruct((T, D), f32), jax....  207 us

profile of v1, /device:TPU:127, one launch (start us, length us, event | category | flops | bytes accessed | tf_op | source)
XLA Modules:
  0.0 213.6 jit_solution(12581411739216405251)
XLA Ops:
  0.6 1.3 fusion
  2.6 206.8 %experts.1 = (f32[128,1152]{1,0:T(8,128)}, bf16[128,1152]{1,0:T(8,128)(2,1)}, bf16[1152,384]{1,0:T(8,128)(2,1)}, bf16[1152,384]{1,0:T(8,128)(2,1)}) custom-call(bf16[128,1152]{1,0:T(8,128)(2,1)} %tok.1, bf16[128,1152]{1,0:T(8,128)(2,1)} %og.1, s32[2,128]{1,0:T(2,128)} %bitcast.4, f32[2,128]{1,0:T(2,128)} %bitcast.5, bf16[1,1152,384]{2,1,0:T(8,128)(2,1)} %win.1, ...), custom_call_target="tpu_custom_call" | custom-call | tf_op jit(solution)/shard_map/experts/pallas_call | solution.py:323
  209.4 0.0 copy-start
  209.4 2.0 add_convert_fusion
  211.4 0.0 copy-done
  211.4 2.2 %select_bitcast_fusion = bf16[1,1152,384]{2,1,0:T(8,128)(2,1)} fusion(bf16[1152,384]{1,0:T(8,128)(2,1)} %get-tuple-element.8, bf16[1152,384]{1,0:T(8,128)(2,1)S(1)} %copy-done, pred[]{:T(512)S(6)} %ne.3), kind=kLoop, calls=%fused_computation | loop fusion | flops 442368 | bytes 2654209 | tf_op jit(solution)/shard_map/broadcast_in_dim | solution.py:369
Async XLA Ops:
  209.4 2.0 copy-start

commit v2 on v1

--- a/solution.py
+++ b/solution.py
@@ -75,15 +75,22 @@
     def put_rows(ref, i, n, value):
         ref[pl.ds(i * n, n)] = value.astype(bf16).reshape(n, B, D)
 
+    z_lo, y, x = e // 16, (e // 4) % 4, e % 4
+
+    def peer(d, sign):
+        a, b = (d // 2) % 4, d // 8
+        to_z, to_y, to_x = d % 2, (a + b) % 4, a
+        return ((z_lo + to_z) % 2) * 16 + ((y + 4 + sign * to_y) % 4) * 4 + (x + 4 + sign * to_x) % 4
+
     def send(src, dst, ss, rs, d):
-        q = (e + d) % E
+        q = peer(d, 1)
         return pltpu.make_async_remote_copy(
             src_ref=at_block(src, q), dst_ref=at_block(dst, e), send_sem=ss.at[d], recv_sem=rs.at[d],
             device_id=(dp, q), device_id_type=MESH,
         )
 
     def arrival(src, dst, ss, rs, d):
-        q = (e + E - d) % E
+        q = peer(d, -1)
         return pltpu.make_async_remote_copy(
             src_ref=at_block(src, q), dst_ref=at_block(dst, q), send_sem=ss.at[d], recv_sem=rs.at[d],
             device_id=(dp, q), device_id_type=MESH,
@@ -294,15 +301,14 @@
 
     for c in copies[4:]:
         c.wait()
-    for i in range(n_chunks - 1):
-        adam(i)
-
+    adam(0)
     wait_all(rg, rt, st, rts, own_r)
     xs[...] = dot(pt[T : 2 * T, :], rows_of(rt, 0, E)).astype(bf16)
     c_back = one(BACK, xs, xr, p_row)
     c_back.start()
     xo[...] = dot(pt[0:T, :], rows_of(rt, 0, E))
-    adam(n_chunks - 1)
+    for i in range(1, n_chunks):
+        adam(i)
 
     @pl.loop(1, E)
     def _(d):

time: 214 us -> 194 us (0.907)
  the two profiles are of different devices: /device:TPU:127 before, /device:TPU:1 now
where the time goes in v2:
time: 194 us; the launch traced here: 193 us
  Pallas kernels  187 us (96%)
  other arithmetic  5.46 us (3%)
    pallas_call x1, Pallas kernels, shards(): pl.pallas_call(kernel, out_shape=(jax.ShapeDtypeStruct((T, D), f32), jax....  187 us

profile of v2, /device:TPU:1, one launch (start us, length us, event | category | flops | bytes accessed | tf_op | source)
XLA Modules:
  0.0 193.5 jit_solution(13895000444112491846)
XLA Ops:
  0.6 1.3 fusion
  2.6 186.7 %experts.1 = (f32[128,1152]{1,0:T(8,128)}, bf16[128,1152]{1,0:T(8,128)(2,1)}, bf16[1152,384]{1,0:T(8,128)(2,1)}, bf16[1152,384]{1,0:T(8,128)(2,1)}) custom-call(bf16[128,1152]{1,0:T(8,128)(2,1)} %tok.1, bf16[128,1152]{1,0:T(8,128)(2,1)} %og.1, s32[2,128]{1,0:T(2,128)} %bitcast.4, f32[2,128]{1,0:T(2,128)} %bitcast.5, bf16[1,1152,384]{2,1,0:T(8,128)(2,1)} %win.1, ...), custom_call_target="tpu_custom_call" | custom-call | tf_op jit(solution)/shard_map/experts/pallas_call | solution.py:329
  189.3 0.0 copy-start
  189.3 2.0 %add_convert_fusion = bf16[128,1152]{1,0:T(8,128)(2,1)} fusion(f32[128,1152]{1,0:T(8,128)} %get-tuple-element.6, bf16[128,1152]{1,0:T(8,128)(2,1)} %get-tuple-element.7), kind=kLoop, calls=%fused_computation.1 | loop fusion | flops 442368 | bytes 1179648 | tf_op jit(solution)/shard_map/convert_element_type | solution.py:372
  191.3 0.0 copy-done
  191.3 2.2 %select_bitcast_fusion = bf16[1,1152,384]{2,1,0:T(8,128)(2,1)} fusion(bf16[1152,384]{1,0:T(8,128)(2,1)} %get-tuple-element.8, bf16[1152,384]{1,0:T(8,128)(2,1)S(1)} %copy-done, pred[]{:T(512)S(6)} %ne.3), kind=kLoop, calls=%fused_computation | loop fusion | flops 442368 | bytes 2654209 | tf_op jit(solution)/shard_map/broadcast_in_dim | solution.py:375
Async XLA Ops:
  189.3 2.0 %copy-start = (bf16[1152,384]{1,0:T(8,128)(2,1)S(1)}, bf16[1152,384]{1,0:T(8,128)(2,1)}, u32[]{:S(2)}) copy-start(bf16[1152,384]{1,0:T(8,128)(2,1)} %get-tuple-element.9) | copy-start | bytes 2654212

commit v3 on v2

v3 whole, which is shorter than its diff:
```python
import jax
import jax.numpy as jnp
from jax import lax
from jax.experimental import pallas as pl
from jax.experimental.pallas import tpu as pltpu
from jax.sharding import PartitionSpec as P

ADAM_STEP = 100
coef_c = 0.7978845608028654
coef_a = 0.044715
beta_one = 0.9
beta_two = 0.999
adam_eps = 1e-08

D = 1152
H = 384
T = 128
E = 32
Q = 16
CAP = 12
B = 2 * CAP
G = Q * B
R = 2 * G
HA, HB = 256, 128
MESH = pl.DeviceIdType.MESH
f32, bf16 = jnp.float32, jnp.bfloat16

OWN, SIB, RA, RAS, RB, RBS = 0, H, 2 * H, 2 * H + HA, 2 * H + 2 * HA, 2 * H + 2 * HA + HB
N_ONE = 40
N_LOCAL = 15


def gelu_slope(u):
    h = jnp.tanh(coef_c * (u + coef_a * u * u * u))
    return 0.5 * (1.0 + h) + 0.5 * u * (1.0 - h * h) * coef_c * (
        1.0 + 3.0 * coef_a * u * u
    )


def dot(a, b):
    return jnp.dot(a, b, preferred_element_type=f32)


def dot_t(a, b):
    return lax.dot_general(a, b, (((1,), (1,)), ((), ())), preferred_element_type=f32)


def kernel(
    tok, og, ids, gts, win, wout, m1, m2,
    xp, xr, ao, ar,
    info, xraw, graw, pk, pt, xpk, gpk, xrv, grv, xt, sl, wi, wo, pg, rg, rt,
    wg, wgr, wsa, wra, wsb, wrb, wsc, wrc, za, zra, zb, zrb, mm1, mm2, zs, zr, xs, keep, an,
    s1, r1, lo, sx, rx, sg, rgs, st, rts,
):
    dp, e = lax.axis_index("dp"), lax.axis_index("expert")
    zh, core = dp // 2, dp % 2
    z_lo, y, x = e // Q, (e // 4) % 4, e % 4
    me = e % Q
    p_row = ((zh + 1 - 2 * (zh % 2)) * 2 + core, e)
    p_wgt = ((3 - zh) * 2 + core, e)
    p_core = (zh * 2 + 1 - core, e)
    p_zlo = (dp, (e + Q) % E)
    used = []
    started = []

    def one(src, dst, dev):
        used.append(None)
        i = len(used) - 1
        return pltpu.make_async_remote_copy(
            src_ref=src, dst_ref=dst, send_sem=s1.at[i], recv_sem=r1.at[i], device_id=dev, device_id_type=MESH
        )

    def go(copy):
        copy.start()
        started.append(copy)

    def local(i, src, dst):
        return pltpu.make_async_copy(src, dst, lo.at[i])

    def rows_of(ref, at, n):
        return ref[pl.ds(at, n)].reshape(n * B, D)

    def put_rows(ref, at, n, value):
        ref[pl.ds(at, n)] = value.astype(bf16).reshape(n, B, D)

    def peer(d, sign):
        a, b = d % 4, d // 4
        return ((y + 4 + sign * ((a + b) % 4)) % 4) * 4 + (x + 4 + sign * a) % 4

    def send(src, dst, ss, rs, g, d):
        q = peer(d, 1)
        return pltpu.make_async_remote_copy(
            src_ref=src.at[g * Q + q], dst_ref=dst.at[g * Q + me], send_sem=ss.at[g * Q + d],
            recv_sem=rs.at[g * Q + d], device_id=(dp, z_lo * Q + q), device_id_type=MESH,
        )

    def arrival(src, dst, ss, rs, g, d):
        q = peer(d, -1)
        return pltpu.make_async_remote_copy(
            src_ref=src.at[g * Q + q], dst_ref=dst.at[g * Q + q], send_sem=ss.at[g * Q + d],
            recv_sem=rs.at[g * Q + d], device_id=(dp, z_lo * Q + q), device_id_type=MESH,
        )

    def own_block(i, src, dst, g):
        return local(i + g, src.at[g * Q + me], dst.at[g * Q + me])

    def send_all(src, dst, ss, rs, g, i):
        own_block(i, src, dst, g).start()

        @pl.loop(1, Q)
        def _(d):
            send(src, dst, ss, rs, g, d).start()

    def wait_all(src, dst, ss, rs, g, i):
        own_block(i, src, dst, g).wait()

        @pl.loop(1, Q)
        def _(d):
            arrival(src, dst, ss, rs, g, d).wait_recv()

    copies = [
        local(0, tok, xraw.at[pl.ds(0, T)]),
        local(1, og, graw.at[pl.ds(0, T)]),
        local(2, win.at[0], wi.at[:, pl.ds(OWN, H)]),
        local(3, wout.at[0], wo.at[pl.ds(OWN, H)]),
        local(4, m1.at[0], mm1),
        local(5, m2.at[0], mm2),
    ]
    for c in copies:
        c.start()

    iota_r = lax.broadcasted_iota(jnp.int32, (T, T), 0)
    iota_c = lax.broadcasted_iota(jnp.int32, (T, T), 1)
    eye, before = iota_r == iota_c, iota_r < iota_c
    idr = [ids[k : k + 1, :].astype(f32) for k in range(2)]

    def to_col(row):
        return jnp.sum(jnp.where(eye, row, 0.0), axis=1, keepdims=True)

    idc = [to_col(r) for r in idr]

    def count(k, j, mask):
        same = idc[k] == idr[j]
        same = jnp.logical_and(same, mask) if mask is not None else same
        return jnp.sum(jnp.where(same, 1.0, 0.0), axis=0, keepdims=True)

    ranks = [count(0, 0, before), count(0, 1, None) + count(1, 1, before)]
    for k in range(2):
        high = jnp.where(idr[k] >= float(Q), 1.0, 0.0)
        info[0, k : k + 1, :] = high * 1024.0 + (idr[k] - high * Q) * float(B) + ranks[k]
    info[0, 2:4, :] = gts[...]
    info[0, 4:8, :] = jnp.zeros((4, T), f32)

    barrier = pltpu.get_barrier_semaphore()
    for dev in (p_row, p_wgt, p_core, p_zlo):
        pl.semaphore_signal(barrier, inc=1, device_id=dev, device_id_type=MESH)

    @pl.loop(1, Q)
    def _(d):
        pl.semaphore_signal(barrier, inc=1, device_id=(dp, z_lo * Q + peer(d, 1)), device_id_type=MESH)

    pl.semaphore_wait(barrier, Q + 3)

    def source(ref, s):
        return ref.at[pl.ds(s * T, T)]

    c_info = [one(info.at[0], info.at[1], p_zlo), one(info.at[0], info.at[2], p_row)]
    c_x = [one(tok, source(xraw, 1), p_zlo), one(tok, source(xraw, 2), p_row)]
    c_g = [one(og, source(graw, 1), p_zlo), one(og, source(graw, 2), p_row)]
    f_info = one(info.at[2], info.at[3], p_zlo)
    f_x = one(source(xraw, 2), source(xraw, 3), p_zlo)
    f_g = one(source(graw, 2), source(graw, 3), p_zlo)

    def columns(ref, at, n):
        return ref.at[:, pl.ds(at, n)]

    def lines(ref, at, n):
        return ref.at[pl.ds(at, n)]

    c_wia = one(win.at[0, :, pl.ds(0, HA)], columns(wi, RA, HA), p_wgt)
    c_woa = one(wout.at[0, pl.ds(0, HA)], lines(wo, RA, HA), p_wgt)
    c_wib = one(win.at[0, :, pl.ds(HA, HB)], columns(wi, RB, HB), p_wgt)
    c_wob = one(wout.at[0, pl.ds(HA, HB)], lines(wo, RB, HB), p_wgt)
    c_wis = one(win.at[0], columns(wi, SIB, H), p_core)
    c_wos = one(wout.at[0], lines(wo, SIB, H), p_core)
    f_wia = one(columns(wi, RA, HA), columns(wi, RAS, HA), p_core)
    f_woa = one(lines(wo, RA, HA), lines(wo, RAS, HA), p_core)
    f_wib = one(columns(wi, RB, HB), columns(wi, RBS, HB), p_core)
    f_wob = one(lines(wo, RB, HB), lines(wo, RBS, HB), p_core)
    for c in [c_info[1], c_x[1], c_info[0], c_x[0], c_g[1], c_g[0], c_wia]:
        go(c)

    def codes(s):
        shift = (s % 2) * CAP - 1024.0 * z_lo.astype(f32)
        return info[s, 0:2, :] + shift

    def build(s):
        code = codes(s)
        g, at = s // 2, s % 2
        row = lax.broadcasted_iota(jnp.int32, (G, T), 0).astype(f32)
        hit = jnp.logical_or(row == code[0:1, :], row == code[1:2, :])
        pk[g * G : (g + 1) * G, at * T : (at + 1) * T] = jnp.where(hit, 1.0, 0.0).astype(bf16)
        lane = lax.broadcasted_iota(jnp.int32, (T, G), 1).astype(f32)
        hit = jnp.logical_or(lane == to_col(code[0:1, :]), lane == to_col(code[1:2, :]))
        pt[s * T : (s + 1) * T, :] = jnp.where(hit, 1.0, 0.0).astype(bf16)

    tile = G // 2

    def pack_x(g):
        raw = xraw[g * 2 * T : (g + 1) * 2 * T, :]
        for i in range(2):
            at = g * G + i * tile
            put_rows(xpk, g * Q + i * Q // 2, Q // 2, dot(pk[at : at + tile, :], raw))

    def pack_g(g):
        raw = graw[g * 2 * T : (g + 1) * 2 * T, :]
        for i in range(2):
            at = g * G + i * tile
            row = (lax.broadcasted_iota(jnp.int32, (tile, T), 0) + i * tile).astype(f32)
            gate = jnp.zeros((tile, T), f32)
            for s in (2 * g, 2 * g + 1):
                code = codes(s)
                for k in range(2):
                    gate += jnp.where(row == code[k : k + 1, :], info[s, 2 + k : 3 + k, :], 0.0)
            gate = jnp.sum(gate, axis=1, keepdims=True)
            put_rows(gpk, g * Q + i * Q // 2, Q // 2, dot(pk[at : at + tile, :], raw) * gate)

    build(0)
    for c in copies[:2]:
        c.wait()
    c_info[0].wait_recv()
    build(1)
    c_x[0].wait_recv()
    pack_x(0)
    send_all(xpk, xrv, sx, rx, 0, 6)
    c_info[1].wait_recv()
    go(f_info)
    c_x[1].wait_recv()
    go(f_x)
    for c in (c_woa, c_wis, c_wos):
        go(c)
    build(2)
    c_g[0].wait_recv()
    pack_g(0)
    send_all(gpk, grv, sg, rgs, 0, 8)
    c_g[1].wait_recv()
    go(f_g)
    for c in (c_wib, c_wob):
        go(c)
    f_info.wait_recv()
    build(3)
    f_x.wait_recv()
    pack_x(1)
    send_all(xpk, xrv, sx, rx, 1, 6)
    f_g.wait_recv()
    pack_g(1)
    send_all(gpk, grv, sg, rgs, 1, 8)

    def slopes(at, n):
        @pl.loop(0, 2)
        def _(g):
            rows = pl.ds(pl.multiple_of(g * G, G), G)
            sl[rows, at : at + n] = gelu_slope(dot(rows_of(xrv, g * Q, Q), wi[:, at : at + n]))

    def grads(at, n, g):
        rows = slice(g * G, (g + 1) * G)
        act = dot_t(rows_of(grv, g * Q, Q), wo[at : at + n, :])
        pg[rows, at : at + n] = (act * sl[rows, at : at + n]).astype(bf16)

    copies[2].wait()
    c_wis.wait_recv()
    for g in range(2):
        wait_all(xpk, xrv, sx, rx, g, 6)
    slopes(OWN, 2 * H)
    xt[...] = rows_of(xrv, 0, 2 * Q).T
    c_wia.wait_recv()
    go(f_wia)
    f_wia.wait_recv()
    slopes(RA, 2 * HA)
    copies[3].wait()
    c_wos.wait_recv()
    wait_all(gpk, grv, sg, rgs, 0, 8)
    grads(OWN, 2 * H, 0)
    c_woa.wait_recv()
    go(f_woa)
    c_wib.wait_recv()
    go(f_wib)
    f_woa.wait_recv()
    grads(RA, 2 * HA, 0)
    f_wib.wait_recv()
    slopes(RB, 2 * HB)
    wait_all(gpk, grv, sg, rgs, 1, 8)
    grads(RA, 2 * HA, 1)

    c_ga = one(wsa, wra, p_core)
    c_gb = one(wsb, wrb, p_core)
    c_gc = one(wsc, wrc, p_core)
    c_za = one(za, zra, p_wgt)
    c_zb = one(zb, zrb, p_wgt)

    def partial_grad(at, n, kept, sent):
        @pl.loop(0, D // H)
        def _(i):
            rows = pl.ds(pl.multiple_of(i * H, H), H)
            part = dot(xt[rows, :], pg[:, at : at + 2 * n])
            kept[rows, :] = part[:, 0:n]
            sent[rows, :] = part[:, n : 2 * n].astype(bf16)

    partial_grad(RA, HA, wgr.at[:, 0:HA], wsa)
    go(c_ga)
    c_wob.wait_recv()
    go(f_wob)
    grads(OWN, 2 * H, 1)
    c_ga.wait_recv()
    za[...] = (wgr[:, 0:HA] + wra[...].astype(f32)).astype(bf16)
    go(c_za)
    f_wob.wait_recv()
    grads(RB, 2 * HB, 1)
    grads(RB, 2 * HB, 0)

    for g in (1, 0):
        put_rows(rg, g * Q, Q, dot_t(pg[g * G : (g + 1) * G, :], wi[...]))
        send_all(rg, rt, st, rts, g, 10)
    partial_grad(RB, HB, wgr.at[:, HA:H], wsb)
    go(c_gb)
    partial_grad(OWN, H, wg, wsc)
    go(c_gc)
    c_gb.wait_recv()
    zb[...] = (wgr[:, HA:H] + wrb[...].astype(f32)).astype(bf16)
    go(c_zb)
    c_gc.wait_recv()
    for c in copies[4:]:
        c.wait()

    def adam(at, n, arrived):
        cols = slice(at, at + n)
        grad = wg[:, cols] + wrc[:, cols].astype(f32) + arrived[...].astype(f32)
        first = beta_one * mm1[:, cols] + (1.0 - beta_one) * grad
        second = beta_two * mm2[:, cols] + (1.0 - beta_two) * grad * grad
        step = (first / (1.0 - beta_one**ADAM_STEP)) / (
            jnp.sqrt(second / (1.0 - beta_two**ADAM_STEP)) + adam_eps
        )
        an[:, cols] = step.astype(bf16)

    c_swa = one(columns(an, 0, HA), columns(ar, 0, HA), p_zlo)
    c_swb = one(columns(an, HA, HB), columns(ar, HA, HB), p_zlo)
    c_z1 = one(zs.at[pl.ds(T, T)], zr.at[pl.ds(T, T)], p_zlo)
    c_z0 = one(zs.at[pl.ds(0, T)], zr.at[pl.ds(0, T)], p_zlo)
    c_back = one(xs, xr, p_row)
    outs = [
        local(12, columns(an, 0, HA), columns(ao, 0, HA)),
        local(13, columns(an, HA, HB), columns(ao, HA, HB)),
        local(14, keep.at[pl.ds(0, T)], xp),
    ]

    def combine(s):
        return dot(pt[s * T : (s + 1) * T, :], rows_of(rt, (s // 2) * Q, Q))

    wait_all(rg, rt, st, rts, 1, 10)
    zs[T : 2 * T, :] = combine(3).astype(bf16)
    go(c_z1)
    keep[T : 2 * T, :] = combine(2)
    wait_all(rg, rt, st, rts, 0, 10)
    zs[0:T, :] = combine(1).astype(bf16)
    go(c_z0)
    keep[0:T, :] = combine(0)
    c_za.wait_recv()
    adam(0, HA, zra)
    c_swa.start()
    outs[0].start()
    c_z1.wait_recv()
    xs[...] = (keep[T : 2 * T, :] + zr[T : 2 * T, :].astype(f32)).astype(bf16)
    c_back.start()
    c_zb.wait_recv()
    adam(HA, HB, zrb)
    c_swb.start()
    outs[1].start()
    c_z0.wait_recv()
    keep[0:T, :] += zr[0:T, :].astype(f32)
    outs[2].start()

    @pl.loop(1, Q)
    def _(d):
        for g in range(2):
            send(xpk, xrv, sx, rx, g, d).wait_send()
            send(gpk, grv, sg, rgs, g, d).wait_send()
            send(rg, rt, st, rts, g, d).wait_send()

    for c in started:
        c.wait_send()
    for c in (c_swa, c_back, c_swb, *outs):
        c.wait()


def finish(swp, xp, xr, an, ar, xo, ao):
    e = lax.axis_index("expert")
    expert = lax.broadcasted_iota(jnp.int32, (1, E), 1)
    new_home = jnp.sum(jnp.where(expert == e, swp[...].astype(f32), 0.0), axis=1, keepdims=True)
    moved = jnp.broadcast_to(new_home != e.astype(f32), (ao.shape[0], T))
    for i in range(0, H, T):
        ao[:, i : i + T] = jnp.where(moved, ar[:, i : i + T], an[:, i : i + T])
    xo[...] = (xp[...] + xr[...].astype(f32)).astype(bf16)


def shards(tokens, out_grad, gates, expert_ids, swap_list, w_in, w_out, first_moment, second_moment):
    any_spec = pl.BlockSpec(memory_space=pl.ANY)
    vmem = pl.BlockSpec(memory_space=pltpu.VMEM)
    dma = pltpu.SemaphoreType.DMA
    xp, xr, an, ar = pl.pallas_call(
        kernel,
        out_shape=(
            jax.ShapeDtypeStruct((T, D), f32),
            jax.ShapeDtypeStruct((T, D), bf16),
            jax.ShapeDtypeStruct((D, H), bf16),
            jax.ShapeDtypeStruct((D, H), bf16),
        ),
        in_specs=[any_spec, any_spec, vmem, vmem, any_spec, any_spec, any_spec, any_spec],
        out_specs=(any_spec, any_spec, any_spec, any_spec),
        scratch_shapes=[
            pltpu.VMEM((4, 8, T), f32),
            pltpu.VMEM((4 * T, D), bf16),
            pltpu.VMEM((4 * T, D), bf16),
            pltpu.VMEM((R, 2 * T), bf16),
            pltpu.VMEM((4 * T, G), bf16),
            pltpu.VMEM((2 * Q, B, D), bf16),
            pltpu.VMEM((2 * Q, B, D), bf16),
            pltpu.VMEM((2 * Q, B, D), bf16),
            pltpu.VMEM((2 * Q, B, D), bf16),
            pltpu.VMEM((D, R), bf16),
            pltpu.VMEM((R, 4 * H), f32),
            pltpu.VMEM((D, 4 * H), bf16),
            pltpu.VMEM((4 * H, D), bf16),
            pltpu.VMEM((R, 4 * H), bf16),
            pltpu.VMEM((2 * Q, B, D), bf16),
            pltpu.VMEM((2 * Q, B, D), bf16),
            pltpu.VMEM((D, H), f32),
            pltpu.VMEM((D, H), f32),
            pltpu.VMEM((D, HA), bf16),
            pltpu.VMEM((D, HA), bf16),
            pltpu.VMEM((D, HB), bf16),
            pltpu.VMEM((D, HB), bf16),
            pltpu.VMEM((D, H), bf16),
            pltpu.VMEM((D, H), bf16),
            pltpu.VMEM((D, HA), bf16),
            pltpu.VMEM((D, HA), bf16),
            pltpu.VMEM((D, HB), bf16),
            pltpu.VMEM((D, HB), bf16),
            pltpu.VMEM((D, H), f32),
            pltpu.VMEM((D, H), f32),
            pltpu.VMEM((2 * T, D), bf16),
            pltpu.VMEM((2 * T, D), bf16),
            pltpu.VMEM((T, D), bf16),
            pltpu.VMEM((2 * T, D), f32),
            pltpu.VMEM((D, H), bf16),
            dma((N_ONE,)), dma((N_ONE,)), dma((N_LOCAL,)),
            dma((E,)), dma((E,)), dma((E,)), dma((E,)), dma((E,)), dma((E,)),
        ],
        compiler_params=pltpu.CompilerParams(
            collective_id=0, has_side_effects=True, vmem_limit_bytes=60 << 20
        ),
        name="experts",
    )(tokens, out_grad, expert_ids.T, gates.T, w_in, w_out, first_moment, second_moment)
    steps = 2
    rows = pl.BlockSpec((T // steps, D), lambda i: (i, 0))
    block = pl.BlockSpec((D // steps, H), lambda i: (i, 0))
    x_grad, adam_out = pl.pallas_call(
        finish,
        grid=(steps,),
        out_shape=(jax.ShapeDtypeStruct((T, D), bf16), jax.ShapeDtypeStruct((D, H), bf16)),
        in_specs=[pl.BlockSpec((1, E), lambda i: (0, 0)), rows, rows, block, block],
        out_specs=(rows, block),
        name="finish",
    )(swap_list[None], xp, xr, an, ar)
    return x_grad, adam_out[None]


def solution(mesh):
    token_spec = P(("dp", "expert"), None)
    in_specs = (
        token_spec, token_spec, token_spec, token_spec, P(),
        P("expert", None, "dp"), P("expert", "dp", None), P("expert", None, "dp"), P("expert", None, "dp"),
    )
    out_specs = (token_spec, P("expert", None, "dp"))
    return jax.shard_map(shards, mesh=mesh, in_specs=in_specs, out_specs=out_specs, check_vma=False)
```

time: 194 us -> 172 us (0.89)
  Pallas kernels: 187 us -> 171 us
  other arithmetic: 5.46 us -> 0 us
    pallas_call x1, Pallas kernels: 187 us -> 168 us  [shards(): pl.pallas_call(kernel, out_shape=(jax.ShapeDtypeStruct((T, D), f32), jax....]
    pallas_call x0 -> x1, Pallas kernels: none -> 2.76 us  [shards(): pl.pallas_call(finish, grid=(steps,), out_shape=(jax.ShapeDtypeStruct((T,...]
    broadcast_in_dim x1 -> x0, other arithmetic: 2.18 us -> none  [shards(): return (x_grad, jnp.where(moved, ar, ao)[None])]
    convert_element_type x1 -> x0, other arithmetic: 1.98 us -> none  [shards(): x_grad = (xo + xr.astype(f32)).astype(bf16)]
where the time goes in v3:
time: 172 us
  Pallas kernels  171 us (99%)
    pallas_call x1, Pallas kernels, shards(): pl.pallas_call(kernel, out_shape=(jax.ShapeDtypeStruct((T, D), f32), jax....  168 us

profile of v3, /device:TPU:1, one launch (start us, length us, event | category | flops | bytes accessed | tf_op | source)
XLA Modules:
  0.0 171.6 jit_solution(8030612738825580136)
XLA Ops:
  0.6 168.2 %experts.1 = (f32[128,1152]{1,0:T(8,128)}, bf16[128,1152]{1,0:T(8,128)(2,1)}, bf16[1152,384]{1,0:T(8,128)(2,1)}, bf16[1152,384]{1,0:T(8,128)(2,1)}) custom-call(bf16[128,1152]{1,0:T(8,128)(2,1)} %tok.1, bf16[128,1152]{1,0:T(8,128)(2,1)} %og.1, s32[2,128]{1,0:T(2,128)} %bitcast.4, f32[2,128]{1,0:T(2,128)} %bitcast.5, bf16[1,1152,384]{2,1,0:T(8,128)(2,1)} %win.1, ...), custom_call_target="tpu_custom_call" | custom-call | tf_op jit(solution)/shard_map/experts/pallas_call | solution.py:409
  168.9 2.8 %finish.1 = (bf16[128,1152]{1,0:T(8,128)(2,1)}, bf16[1152,384]{1,0:T(8,128)(2,1)}) custom-call(s32[1,32]{1,0:T(1,128)} %bitcast.6, f32[128,1152]{1,0:T(8,128)} %get-tuple-element.8.xp, bf16[128,1152]{1,0:T(8,128)(2,1)} %get-tuple-element.9.xr, bf16[1152,384]{1,0:T(8,128)(2,1)} %get-tuple-element.10.an, bf16[1152,384]{1,0:T(8,128)(2,1)} %get-tuple-element.11.ar), custom_call_target="tpu_custom_call" | custom-call | tf_op jit(solution)/shard_map/finish/pallas_call | solution.py:466

commit v4 on v3

--- a/solution.py
+++ b/solution.py
@@ -49,7 +49,7 @@
     tok, og, ids, gts, win, wout, m1, m2,
     xp, xr, ao, ar,
     info, xraw, graw, pk, pt, xpk, gpk, xrv, grv, xt, sl, wi, wo, pg, rg, rt,
-    wg, wgr, wsa, wra, wsb, wrb, wsc, wrc, za, zra, zb, zrb, mm1, mm2, zs, zr, xs, keep, an,
+    wg, wgr, wsa, wra, wsb, wrb, wsc, wrc, za, zra, zb, zrb, mm1, mm2, zs, zr, zd, xs, keep, an,
     s1, r1, lo, sx, rx, sg, rgs, st, rts,
 ):
     dp, e = lax.axis_index("dp"), lax.axis_index("expert")
@@ -60,6 +60,9 @@
     p_wgt = ((3 - zh) * 2 + core, e)
     p_core = (zh * 2 + 1 - core, e)
     p_zlo = (dp, (e + Q) % E)
+    p_diag = ((zh + 1 - 2 * (zh % 2)) * 2 + core, (e + Q) % E)
+    inner = (zh % 2 + z_lo) == 1
+    outer = (zh % 2 + z_lo) != 1
     used = []
     started = []
 
@@ -152,14 +155,14 @@
     info[0, 4:8, :] = jnp.zeros((4, T), f32)
 
     barrier = pltpu.get_barrier_semaphore()
-    for dev in (p_row, p_wgt, p_core, p_zlo):
+    for dev in (p_row, p_wgt, p_core, p_zlo, p_diag):
         pl.semaphore_signal(barrier, inc=1, device_id=dev, device_id_type=MESH)
 
     @pl.loop(1, Q)
     def _(d):
         pl.semaphore_signal(barrier, inc=1, device_id=(dp, z_lo * Q + peer(d, 1)), device_id_type=MESH)
 
-    pl.semaphore_wait(barrier, Q + 3)
+    pl.semaphore_wait(barrier, Q + 4)
 
     def source(ref, s):
         return ref.at[pl.ds(s * T, T)]
@@ -170,6 +173,25 @@
     f_info = one(info.at[2], info.at[3], p_zlo)
     f_x = one(source(xraw, 2), source(xraw, 3), p_zlo)
     f_g = one(source(graw, 2), source(graw, 3), p_zlo)
+
+    d_info = one(info.at[0], info.at[3], p_diag)
+    d_x = one(tok, source(xraw, 3), p_diag)
+    d_g = one(og, source(graw, 3), p_diag)
+
+    def inner_go(*copies_out):
+        @pl.when(inner)
+        def _():
+            for c in copies_out:
+                c.start()
+
+    def wait_diag(direct, passed):
+        @pl.when(inner)
+        def _():
+            direct.wait_recv()
+
+        @pl.when(outer)
+        def _():
+            passed.wait_recv()
 
     def columns(ref, at, n):
         return ref.at[:, pl.ds(at, n)]
@@ -187,8 +209,10 @@
     f_woa = one(lines(wo, RA, HA), lines(wo, RAS, HA), p_core)
     f_wib = one(columns(wi, RB, HB), columns(wi, RBS, HB), p_core)
     f_wob = one(lines(wo, RB, HB), lines(wo, RBS, HB), p_core)
-    for c in [c_info[1], c_x[1], c_info[0], c_x[0], c_g[1], c_g[0], c_wia]:
+    for c in [c_info[1], c_x[1], c_info[0], c_x[0], c_g[1], c_g[0]]:
         go(c)
+    inner_go(d_info, d_x, d_g)
+    go(c_wia)
 
     def codes(s):
         shift = (s % 2) * CAP - 1024.0 * z_lo.astype(f32)
@@ -234,9 +258,9 @@
     pack_x(0)
     send_all(xpk, xrv, sx, rx, 0, 6)
     c_info[1].wait_recv()
-    go(f_info)
+    inner_go(f_info)
     c_x[1].wait_recv()
-    go(f_x)
+    inner_go(f_x)
     for c in (c_woa, c_wis, c_wos):
         go(c)
     build(2)
@@ -244,15 +268,15 @@
     pack_g(0)
     send_all(gpk, grv, sg, rgs, 0, 8)
     c_g[1].wait_recv()
-    go(f_g)
+    inner_go(f_g)
     for c in (c_wib, c_wob):
         go(c)
-    f_info.wait_recv()
+    wait_diag(d_info, f_info)
     build(3)
-    f_x.wait_recv()
+    wait_diag(d_x, f_x)
     pack_x(1)
     send_all(xpk, xrv, sx, rx, 1, 6)
-    f_g.wait_recv()
+    wait_diag(d_g, f_g)
     pack_g(1)
     send_all(gpk, grv, sg, rgs, 1, 8)
 
@@ -345,6 +369,7 @@
     c_swa = one(columns(an, 0, HA), columns(ar, 0, HA), p_zlo)
     c_swb = one(columns(an, HA, HB), columns(ar, HA, HB), p_zlo)
     c_z1 = one(zs.at[pl.ds(T, T)], zr.at[pl.ds(T, T)], p_zlo)
+    c_zd = one(zs.at[pl.ds(T, T)], zd, p_diag)
     c_z0 = one(zs.at[pl.ds(0, T)], zr.at[pl.ds(0, T)], p_zlo)
     c_back = one(xs, xr, p_row)
     outs = [
@@ -358,8 +383,22 @@
 
     wait_all(rg, rt, st, rts, 1, 10)
     zs[T : 2 * T, :] = combine(3).astype(bf16)
-    go(c_z1)
+
+    @pl.when(inner)
+    def _():
+        c_zd.start()
+
+    @pl.when(outer)
+    def _():
+        c_z1.start()
+
     keep[T : 2 * T, :] = combine(2)
+
+    @pl.when(outer)
+    def _():
+        xs[...] = keep[T : 2 * T, :].astype(bf16)
+        c_back.start()
+
     wait_all(rg, rt, st, rts, 0, 10)
     zs[0:T, :] = combine(1).astype(bf16)
     go(c_z0)
@@ -368,15 +407,25 @@
     adam(0, HA, zra)
     c_swa.start()
     outs[0].start()
-    c_z1.wait_recv()
-    xs[...] = (keep[T : 2 * T, :] + zr[T : 2 * T, :].astype(f32)).astype(bf16)
-    c_back.start()
+
+    @pl.when(inner)
+    def _():
+        c_z1.wait_recv()
+        xs[...] = (keep[T : 2 * T, :] + zr[T : 2 * T, :].astype(f32)).astype(bf16)
+        c_back.start()
+
     c_zb.wait_recv()
     adam(HA, HB, zrb)
     c_swb.start()
     outs[1].start()
     c_z0.wait_recv()
     keep[0:T, :] += zr[0:T, :].astype(f32)
+
+    @pl.when(inner)
+    def _():
+        c_zd.wait_recv()
+        keep[0:T, :] += zd[...].astype(f32)
+
     outs[2].start()
 
     @pl.loop(1, Q)
@@ -388,6 +437,16 @@
 
     for c in started:
         c.wait_send()
+
+    @pl.when(inner)
+    def _():
+        for c in (d_info, d_x, d_g, f_info, f_x, f_g, c_zd):
+            c.wait_send()
+
+    @pl.when(outer)
+    def _():
+        c_z1.wait_send()
+
     for c in (c_swa, c_back, c_swb, *outs):
         c.wait()
 
@@ -450,6 +509,7 @@
             pltpu.VMEM((2 * T, D), bf16),
             pltpu.VMEM((2 * T, D), bf16),
             pltpu.VMEM((T, D), bf16),
+            pltpu.VMEM((T, D), bf16),
             pltpu.VMEM((2 * T, D), f32),
             pltpu.VMEM((D, H), bf16),
             dma((N_ONE,)), dma((N_ONE,)), dma((N_LOCAL,)),

time: 172 us -> 168 us (0.977)
  Pallas kernels: 171 us -> 167 us
    pallas_call x1, Pallas kernels: 168 us -> 164 us  [shards(): pl.pallas_call(kernel, out_shape=(jax.ShapeDtypeStruct((T, D), f32), jax....]
where the time goes in v4:
time: 168 us
  Pallas kernels  167 us (99%)
    pallas_call x1, Pallas kernels, shards(): pl.pallas_call(kernel, out_shape=(jax.ShapeDtypeStruct((T, D), f32), jax....  164 us

profile of v4, /device:TPU:1, one launch (start us, length us, event | category | flops | bytes accessed | tf_op | source)
XLA Modules:
  0.0 167.8 jit_solution(7567640589694358847)
XLA Ops:
  0.6 164.4 %experts.1 = (f32[128,1152]{1,0:T(8,128)}, bf16[128,1152]{1,0:T(8,128)(2,1)}, bf16[1152,384]{1,0:T(8,128)(2,1)}, bf16[1152,384]{1,0:T(8,128)(2,1)}) custom-call(bf16[128,1152]{1,0:T(8,128)(2,1)} %tok.1, bf16[128,1152]{1,0:T(8,128)(2,1)} %og.1, s32[2,128]{1,0:T(2,128)} %bitcast.4, f32[2,128]{1,0:T(2,128)} %bitcast.5, bf16[1,1152,384]{2,1,0:T(8,128)(2,1)} %win.1, ...), custom_call_target="tpu_custom_call" | custom-call | tf_op jit(solution)/shard_map/experts/pallas_call | solution.py:468
  165.0 2.8 %finish.1 = (bf16[128,1152]{1,0:T(8,128)(2,1)}, bf16[1152,384]{1,0:T(8,128)(2,1)}) custom-call(s32[1,32]{1,0:T(1,128)} %bitcast.6, f32[128,1152]{1,0:T(8,128)} %get-tuple-element.8.xp, bf16[128,1152]{1,0:T(8,128)(2,1)} %get-tuple-element.9.xr, bf16[1152,384]{1,0:T(8,128)(2,1)} %get-tuple-element.10.an, bf16[1152,384]{1,0:T(8,128)(2,1)} %get-tuple-element.11.ar), custom_call_target="tpu_custom_call" | custom-call | tf_op jit(solution)/shard_map/finish/pallas_call | solution.py:526

commit v5 on v4

--- a/solution.py
+++ b/solution.py
@@ -403,16 +403,17 @@
     zs[0:T, :] = combine(1).astype(bf16)
     go(c_z0)
     keep[0:T, :] = combine(0)
+
+    @pl.when(inner)
+    def _():
+        c_z1.wait_recv()
+        xs[...] = (keep[T : 2 * T, :] + zr[T : 2 * T, :].astype(f32)).astype(bf16)
+        c_back.start()
+
     c_za.wait_recv()
     adam(0, HA, zra)
     c_swa.start()
     outs[0].start()
-
-    @pl.when(inner)
-    def _():
-        c_z1.wait_recv()
-        xs[...] = (keep[T : 2 * T, :] + zr[T : 2 * T, :].astype(f32)).astype(bf16)
-        c_back.start()
 
     c_zb.wait_recv()
     adam(HA, HB, zrb)

time: 168 us -> 168 us (level)
  no operation moved by 1% of the time
where the time goes in v5:
time: 168 us
  Pallas kernels  167 us (99%)
    pallas_call x1, Pallas kernels, shards(): pl.pallas_call(kernel, out_shape=(jax.ShapeDtypeStruct((T, D), f32), jax....  164 us

profile of v5, /device:TPU:1, one launch (start us, length us, event | category | flops | bytes accessed | tf_op | source)
XLA Modules:
  0.0 167.8 jit_solution(16220514108617635374)
XLA Ops:
  0.6 164.4 %experts.1 = (f32[128,1152]{1,0:T(8,128)}, bf16[128,1152]{1,0:T(8,128)(2,1)}, bf16[1152,384]{1,0:T(8,128)(2,1)}, bf16[1152,384]{1,0:T(8,128)(2,1)}) custom-call(bf16[128,1152]{1,0:T(8,128)(2,1)} %tok.1, bf16[128,1152]{1,0:T(8,128)(2,1)} %og.1, s32[2,128]{1,0:T(2,128)} %bitcast.4, f32[2,128]{1,0:T(2,128)} %bitcast.5, bf16[1,1152,384]{2,1,0:T(8,128)(2,1)} %win.1, ...), custom_call_target="tpu_custom_call" | custom-call | tf_op jit(solution)/shard_map/experts/pallas_call | solution.py:469
  165.0 2.8 %finish.1 = (bf16[128,1152]{1,0:T(8,128)(2,1)}, bf16[1152,384]{1,0:T(8,128)(2,1)}) custom-call(s32[1,32]{1,0:T(1,128)} %bitcast.6, f32[128,1152]{1,0:T(8,128)} %get-tuple-element.8.xp, bf16[128,1152]{1,0:T(8,128)(2,1)} %get-tuple-element.9.xr, bf16[1152,384]{1,0:T(8,128)(2,1)} %get-tuple-element.10.an, bf16[1152,384]{1,0:T(8,128)(2,1)} %get-tuple-element.11.ar), custom_call_target="tpu_custom_call" | custom-call | tf_op jit(solution)/shard_map/finish/pallas_call | solution.py:527
